TPU v7x, 32 devices: a whole 2x2x4 slice. The times are simulated.
32 devices in a mesh: ctx: 16 (over z, y, core), ch: 2 (over x).
Axes of the slice: x: 2, y: 2, z: 4, core: 2. Of those that a mesh axis runs over, the one named last changes fastest.
Arguments:
- inputs: float32 [12288, 2048], P('ctx', 'ch'), may hold values from -6 to 6
- cotangent: float32 [12288, 2048], P('ctx', 'ch'), may hold values from -6 to 6
- filter_rows: float32 [1536, 2048], P('ctx', 'ch'), may hold values from -0.15625 to 0.15625
- skip_gain: float32 [2048], P('ch'), may hold values from -1 to 1
- band_blocks: int32 [2048], P('ch'), may hold values from 1 to 2
Outputs:
- outputs: float32 [12288, 2048], P('ctx', 'ch')
- input_grad: float32 [2048, 12288], P(('ch', 'ctx'))
All inputs are finite; a program needn't handle non-finite values.
Results may differ from a plain program's by a relative error of at most 0.00007.
Values sent between devices are 32-bit elements; how exact they have to be, the bound alone decides.
A program may use at most 192 MiB of HBM per device.

v0:
```python
import math

import jax
import jax.numpy as jnp
from jax import lax
from jax.sharding import PartitionSpec as P

PRECISE = lax.Precision.HIGHEST


def passed_along(value, axis, steps):
    count = lax.axis_size(axis)
    initial, last = (max(0, -steps), min(count, count - steps))
    return lax.ppermute(value, axis, [(source, source + steps) for source in range(initial, last)])


def factor_pair(length):
    leading = 1
    candidate = 1
    while candidate * candidate <= length:
        if length % candidate == 0:
            leading = candidate
        candidate += 1
    return (leading, length // leading)


def twiddle_table(row_count, col_count, period, direction):
    product = (
        jnp.arange(row_count, dtype=jnp.int32)[:, None]
        * jnp.arange(col_count, dtype=jnp.int32)[None, :]
        % period
    )
    angle_val = product.astype(jnp.float32) * (2.0 * math.pi / period)
    return (jnp.cos(angle_val), direction * jnp.sin(angle_val))


def forward_real(signal, factors):
    leading, trailing = factors
    length = leading * trailing
    kept = trailing // 2 + 1
    grid_view = signal.reshape(leading, trailing, signal.shape[-1])
    cos_first, sin_first = twiddle_table(leading, leading, leading, -1.0)
    section_real = jnp.einsum("kn,nmc->kmc", cos_first, grid_view, precision=PRECISE)
    section_imag = jnp.einsum("kn,nmc->kmc", sin_first, grid_view, precision=PRECISE)
    turn_real, turn_imag = twiddle_table(leading, trailing, length, -1.0)
    rot_real = section_real * turn_real[:, :, None] - section_imag * turn_imag[:, :, None]
    rot_imag = section_real * turn_imag[:, :, None] + section_imag * turn_real[:, :, None]
    cos_second, sin_second = twiddle_table(trailing, kept, trailing, -1.0)
    out_real = jnp.einsum("kmc,mj->kjc", rot_real, cos_second, precision=PRECISE) - jnp.einsum(
        "kmc,mj->kjc", rot_imag, sin_second, precision=PRECISE
    )
    out_imag = jnp.einsum("kmc,mj->kjc", rot_real, sin_second, precision=PRECISE) + jnp.einsum(
        "kmc,mj->kjc", rot_imag, cos_second, precision=PRECISE
    )
    return jnp.stack([out_real, out_imag])


def inverse_real(spectrum, factors, channel_major):
    leading, trailing = factors
    length = leading * trailing
    kept = trailing // 2 + 1
    freq_index = (
        jnp.arange(leading, dtype=jnp.int32)[:, None]
        + leading * jnp.arange(kept, dtype=jnp.int32)[None, :]
    )
    edge_bin = (freq_index == 0) | (2 * freq_index == length)
    weights = jnp.where(edge_bin, 1.0, jnp.where(2 * freq_index < length, 2.0, 0.0)).astype(
        jnp.float32
    )
    spec_real = spectrum[0] * weights[:, :, None]
    spec_imag = spectrum[1] * weights[:, :, None]
    cos_second, sin_second = twiddle_table(kept, trailing, trailing, 1.0)
    part_real = jnp.einsum("kjc,jm->kmc", spec_real, cos_second, precision=PRECISE) - jnp.einsum(
        "kjc,jm->kmc", spec_imag, sin_second, precision=PRECISE
    )
    part_imag = jnp.einsum("kjc,jm->kmc", spec_real, sin_second, precision=PRECISE) + jnp.einsum(
        "kjc,jm->kmc", spec_imag, cos_second, precision=PRECISE
    )
    turn_real, turn_imag = twiddle_table(leading, trailing, length, 1.0)
    rot_real = part_real * turn_real[:, :, None] - part_imag * turn_imag[:, :, None]
    rot_imag = part_real * turn_imag[:, :, None] + part_imag * turn_real[:, :, None]
    cos_first, sin_first = twiddle_table(leading, leading, leading, 1.0)
    if channel_major:
        result = jnp.einsum("nk,kmc->cnm", cos_first, rot_real, precision=PRECISE) - jnp.einsum(
            "nk,kmc->cnm", sin_first, rot_imag, precision=PRECISE
        )
        return result.reshape(result.shape[0], length) / length
    result = jnp.einsum("nk,kmc->nmc", cos_first, rot_real, precision=PRECISE) - jnp.einsum(
        "nk,kmc->nmc", sin_first, rot_imag, precision=PRECISE
    )
    return result.reshape(length, result.shape[-1]) / length


def spectral_product(tap_spec, panel_spec, conjugate):
    tap_real, tap_imag = (tap_spec[0], tap_spec[1])
    if conjugate:
        tap_imag = -tap_imag
    panel_real, panel_imag = (panel_spec[0], panel_spec[1])
    return jnp.stack(
        [
            tap_real * panel_real - tap_imag * panel_imag,
            tap_real * panel_imag + tap_imag * panel_real,
        ]
    )


def local(inputs, cotangent, filter_rows, skip_gain, band_blocks):
    block_len = inputs.shape[0]
    factors = factor_pair(2 * block_len)
    piece_rows = lax.all_gather(filter_rows, "ctx", axis=0, tiled=True)
    lag_index = jnp.arange(piece_rows.shape[0], dtype=jnp.int32)
    keep_mask = lag_index[:, None] < band_blocks[None, :] * block_len
    filter_full = jnp.where(keep_mask, piece_rows, jnp.zeros_like(piece_rows))
    lag_zero = jnp.arange(filter_full.shape[0], dtype=jnp.int32)[:, None] == 0
    filter_full = filter_full + jnp.where(lag_zero, skip_gain[None, :], 0.0)
    blank_rows = jnp.zeros_like(inputs)
    lower_one = passed_along(inputs, "ctx", 1)
    upper_one = passed_along(cotangent, "ctx", -1)
    own_forward = forward_real(jnp.concatenate([lower_one, inputs], axis=0), factors)
    own_backward = forward_real(jnp.concatenate([cotangent, upper_one], axis=0), factors)
    forward_sources = [own_forward]
    backward_sources = [own_backward]
    lag_block = 1
    forward_sources.append(passed_along(own_forward, "ctx", lag_block))
    backward_sources.append(passed_along(own_backward, "ctx", -lag_block))

    def tile_terms(totals, lag_block):
        tap_block = lax.slice_in_dim(
            filter_full, lag_block * block_len, (lag_block + 1) * block_len, axis=0
        )
        tap_spec = forward_real(jnp.concatenate([tap_block, blank_rows], axis=0), factors)
        forward_panel = forward_sources[lag_block]
        backward_panel = backward_sources[lag_block]
        return (
            totals[0] + spectral_product(tap_spec, forward_panel, False),
            totals[1] + spectral_product(tap_spec, backward_panel, True),
        )

    totals = tile_terms((0.0, 0.0), 0)
    lag_block = 1
    totals = tile_terms(totals, lag_block)
    forward_time = inverse_real(totals[0], factors, False)
    outputs = lax.slice_in_dim(forward_time, block_len, 2 * block_len, axis=0)
    backward_time = inverse_real(totals[1], factors, True)
    local_grad = lax.slice_in_dim(backward_time, 0, block_len, axis=1)
    input_grad = lax.all_to_all(local_grad, "ctx", split_axis=0, concat_axis=1, tiled=True)
    return (outputs, input_grad)


def solution(mesh):
    return jax.shard_map(
        local,
        mesh=mesh,
        in_specs=(P("ctx", "ch"), P("ctx", "ch"), P("ctx", "ch"), P("ch"), P("ch")),
        out_specs=(P("ctx", "ch"), P(("ch", "ctx"), None)),
        check_vma=False,
    )
```

profile of v0, /device:TPU:13, one launch (start us, length us, event | category | flops | bytes accessed | tf_op | source)
XLA Modules:
  0.0 701.2 jit_solution(13089642921306606010)
XLA Ops:
  15.2 59.7 %collective-permute-done.2 = f32[768,1024]{1,0:T(8,128)S(1)} collective-permute-done((f32[768,1024]{1,0:T(8,128)}, f32[768,1024]{1,0:T(8,128)S(1)}, u32[]{:S(2)}, u32[]{:S(2)}) %collective-permute-start.2) | collective-permute-done | bytes 3145760 | tf_op jit(solution)/shard_map/ppermute | solution.py:14
  78.9 10.0 %fusion.44 = f32[32,48,1024]{2,0,1:T(8,128)} fusion(f32[32,48,1024]{2,1,0:T(8,128)S(1)} %bitcast.317), kind=kOutput, calls=%fused_computation.69 | convolution fusion | flops 603995136 | bytes 12582912 | tf_op jit(solution)/shard_map/kn,nmc->kmc/dot_general | solution.py:44
  88.9 10.1 %fusion.46 = f32[32,48,1024]{2,0,1:T(8,128)} fusion(f32[32,48,1024]{2,1,0:T(8,128)S(1)} %bitcast.318), kind=kOutput, calls=%fused_computation.71 | convolution fusion | flops 603994112 | bytes 12582912 | tf_op jit(solution)/shard_map/kn,nmc->kmc/dot_general | solution.py:43
  99.0 10.3 %fusion.22 = f32[32,48,1024]{2,0,1:T(8,128)} fusion(f32[32,48,1024]{2,1,0:T(8,128)S(1)} %bitcast.303), kind=kOutput, calls=%fused_computation.47 | convolution fusion | flops 603994112 | bytes 12582912 | tf_op jit(solution)/shard_map/kn,nmc->kmc/dot_general | solution.py:43
  114.5 10.1 %fusion.32 = f32[32,48,1024]{2,0,1:T(8,128)} fusion(f32[32,48,1024]{2,1,0:T(8,128)S(1)} %bitcast.315), kind=kOutput, calls=%fused_computation.57 | convolution fusion | flops 603995136 | bytes 12582912 | tf_op jit(solution)/shard_map/kn,nmc->kmc/dot_general | solution.py:44
  124.6 10.4 %fusion.34 = f32[32,48,1024]{2,0,1:T(8,128)} fusion(f32[32,48,1024]{2,1,0:T(8,128)S(1)} %bitcast.316), kind=kOutput, calls=%fused_computation.59 | convolution fusion | flops 603994112 | bytes 12582912 | tf_op jit(solution)/shard_map/kn,nmc->kmc/dot_general | solution.py:43
  135.0 10.1 %fusion.56 = f32[32,48,1024]{2,0,1:T(8,128)} fusion(f32[32,48,1024]{2,1,0:T(8,128)S(1)} %bitcast.313), kind=kOutput, calls=%fused_computation.81 | convolution fusion | flops 603995136 | bytes 12582912 | tf_op jit(solution)/shard_map/kn,nmc->kmc/dot_general | solution.py:44
  145.1 10.3 %fusion.58 = f32[32,48,1024]{2,0,1:T(8,128)} fusion(f32[32,48,1024]{2,1,0:T(8,128)S(1)} %bitcast.314), kind=kOutput, calls=%fused_computation.83 | convolution fusion | flops 603994112 | bytes 12582912 | tf_op jit(solution)/shard_map/kn,nmc->kmc/dot_general | solution.py:43
  155.4 40.5 %multiply_subtract_fusion = (f32[32,48,1024]{2,0,1:T(8,128)}, f32[32,48,1024]{2,0,1:T(8,128)}, f32[32,48,1024]{2,0,1:T(8,128)}, f32[32,48,1024]{2,0,1:T(8,128)},...) fusion(f32[32,48,1024]{2,0,1:T(8,128)} %fusion.22, ...), kind=kOutput, calls=%fused_computation.28 | convolution fusion | flops 641743872 | bytes 100675584 | tf_op jit(solution)/shard_map/kn,nmc->kmc/dot_general | solution.py:44
  195.9 10.7 %fusion.12 = f32[25,32,1024]{2,0,1:T(8,128)S(1)} fusion(f32[32,48,1024]{2,0,1:T(8,128)} %get-tuple-element.13), kind=kOutput, calls=%fused_computation.37 | convolution fusion | flops 471870016 | bytes 9568256 | tf_op jit(solution)/shard_map/kmc,mj->kjc/dot_general | solution.py:52
  206.7 8.2 %fusion.14 = f32[25,32,1024]{2,0,1:T(8,128)} fusion(f32[32,48,1024]{2,0,1:T(8,128)S(1)} %copy-done.1), kind=kOutput, calls=%fused_computation.39 | convolution fusion | flops 471871200 | bytes 9568256 | tf_op jit(solution)/shard_map/kmc,mj->kjc/dot_general | solution.py:49
  214.9 8.6 %fusion.38 = f32[25,32,1024]{2,0,1:T(8,128)} fusion(f32[32,48,1024]{2,0,1:T(8,128)S(1)} %bitcast.306), kind=kOutput, calls=%fused_computation.63 | convolution fusion | flops 471871200 | bytes 9568256 | tf_op jit(solution)/shard_map/kmc,mj->kjc/dot_general | solution.py:49
  231.6 8.4 %fusion.136 = f32[25,32,1024]{2,0,1:T(8,128)S(1)} fusion(f32[25,32,1024]{2,0,1:T(8,128)S(1)} %fusion.12, f32[32,48,1024]{2,0,1:T(8,128)S(1)} %bitcast.298), kind=kOutput, calls=%fused_computation.157 | convolution fusion | flops 472690400 | bytes 12845056 | tf_op jit(solution)/shard_map/kmc,mj->kjc/dot_general | solution.py:52
  240.1 8.1 %fusion.133 = f32[25,32,1024]{2,0,1:T(8,128)S(1)} fusion(f32[25,32,1024]{2,0,1:T(8,128)S(1)} %copy-done.6, f32[32,48,1024]{2,0,1:T(8,128)S(1)} %bitcast.298), kind=kOutput, calls=%fused_computation.156 | convolution fusion | flops 472689216 | bytes 12845056 | tf_op jit(solution)/shard_map/kmc,mj->kjc/dot_general | solution.py:49
  252.9 10.3 %copy.136 = f32[2,32,25,1024]{3,1,2,0:T(8,128)} copy(f32[2,32,25,1024]{3,2,1,0:T(8,128)} %pad_maximum_fusion.1) | data formatting | bytes 13107200 | tf_op jit(solution)/shard_map/stack | solution.py:55
  263.1 27.4 %collective-permute-start.3 = (f32[2,32,25,1024]{3,1,2,0:T(8,128)}, f32[2,32,25,1024]{3,1,2,0:T(8,128)}, u32[]{:S(2)}, u32[]{:S(2)}) collective-permute-start(f32[2,32,25,1024]{3,1,2,0:T(8,128)} %copy.136), channel_id=1, source_target_pairs={{2,0},{4,2},{6,4},{8,6},{10,8},{12,10},{14,12},{16,14},{18,16},{20... | collective-permute-start | bytes 19660808 | tf_op jit(solution)/shard_map/ppermute | solution.py:14
  290.5 8.1 %fusion.121 = f32[25,32,1024]{2,0,1:T(8,128)S(1)} fusion(f32[25,32,1024]{2,0,1:T(8,128)S(1)} %copy-done.5, f32[32,48,1024]{2,0,1:T(8,128)S(1)} %bitcast.296), kind=kOutput, calls=%fused_computation.152 | convolution fusion | flops 472689216 | bytes 12845056 | tf_op jit(solution)/shard_map/kmc,mj->kjc/dot_general | solution.py:49
  298.7 8.8 %fusion.124 = f32[25,32,1024]{2,0,1:T(8,128)} fusion(f32[25,32,1024]{2,0,1:T(8,128)S(1)} %fusion.36, f32[32,48,1024]{2,0,1:T(8,128)S(1)} %bitcast.296), kind=kOutput, calls=%fused_computation.153 | convolution fusion | flops 472690400 | bytes 12845056 | tf_op jit(solution)/shard_map/kmc,mj->kjc/dot_general | solution.py:52
  314.5 9.9 %copy.120 = f32[2,32,25,1024]{3,1,2,0:T(8,128)} copy(f32[2,32,25,1024]{3,2,1,0:T(8,128)} %pad_maximum_fusion) | data formatting | bytes 13107200 | tf_op jit(solution)/shard_map/stack | solution.py:55
  326.7 8.1 %fusion.48 = f32[25,32,1024]{2,0,1:T(8,128)S(1)} fusion(f32[32,48,1024]{2,0,1:T(8,128)S(1)} %bitcast.302), kind=kOutput, calls=%fused_computation.73 | convolution fusion | flops 471870016 | bytes 9568256 | tf_op jit(solution)/shard_map/kmc,mj->kjc/dot_general | solution.py:52
  334.7 8.4 %fusion.50 = f32[25,32,1024]{2,0,1:T(8,128)} fusion(f32[32,48,1024]{2,0,1:T(8,128)S(1)} %bitcast.302), kind=kOutput, calls=%fused_computation.75 | convolution fusion | flops 471871200 | bytes 9568256 | tf_op jit(solution)/shard_map/kmc,mj->kjc/dot_general | solution.py:49
  343.2 8.1 %fusion.24 = f32[25,32,1024]{2,0,1:T(8,128)S(1)} fusion(f32[32,48,1024]{2,0,1:T(8,128)S(1)} %bitcast.300), kind=kOutput, calls=%fused_computation.49 | convolution fusion | flops 471870016 | bytes 9568256 | tf_op jit(solution)/shard_map/kmc,mj->kjc/dot_general | solution.py:52
  351.3 8.5 %fusion.26 = f32[25,32,1024]{2,0,1:T(8,128)} fusion(f32[32,48,1024]{2,0,1:T(8,128)S(1)} %bitcast.300), kind=kOutput, calls=%fused_computation.51 | convolution fusion | flops 471871200 | bytes 9568256 | tf_op jit(solution)/shard_map/kmc,mj->kjc/dot_general | solution.py:49
  359.8 8.4 %fusion.118 = f32[25,32,1024]{2,0,1:T(8,128)} fusion(f32[25,32,1024]{2,0,1:T(8,128)S(1)} %fusion.48, f32[32,48,1024]{2,0,1:T(8,128)S(1)} %bitcast.312), kind=kOutput, calls=%fused_computation.151 | convolution fusion | flops 472690400 | bytes 12845056 | tf_op jit(solution)/shard_map/kmc,mj->kjc/dot_general | solution.py:52
  368.1 8.4 %fusion.130 = f32[25,32,1024]{2,0,1:T(8,128)} fusion(f32[25,32,1024]{2,0,1:T(8,128)S(1)} %fusion.24, f32[32,48,1024]{2,0,1:T(8,128)S(1)} %bitcast.308), kind=kOutput, calls=%fused_computation.155 | convolution fusion | flops 472690400 | bytes 12845056 | tf_op jit(solution)/shard_map/kmc,mj->kjc/dot_general | solution.py:52
  376.5 19.3 %fusion.81 = (f32[1,32,25,1024]{3,2,1,0:T(8,128)}, f32[1,32,25,1024]{3,2,1,0:T(8,128)}, f32[1,32,25,1024]{3,2,1,0:T(8,128)}, f32[1,32,25,1024]{3,2,1,0:T(8,128)}) fusion(f32[25,32,1024]{2,0,1:T(8,128)S(1)} %fusion.136, f32[25,32,1024]{2,0,1:T(8,128)} %copy-done.3, f32[25,32,1024]{2,0,1:T(8,128)} %fusion.118, f32[25,32,1024]{2,0,1:T(8,128)} %copy-done.4, ...), kind=kOutput, calls=%fused_computation.116 | convolution fusion | flops 483338816 | bytes 39059456 | tf_op jit(solution)/shard_map/kmc,mj->kjc/dot_general | solution.py:49
  409.9 24.6 %fusion.67 = (f32[1,32,25,1024]{3,2,1,0:T(8,128)}, f32[1,32,25,1024]{3,2,1,0:T(8,128)}, f32[1,32,25,1024]{3,2,1,0:T(8,128)}, f32[1,32,25,1024]{3,2,1,0:T(8,128)}) fusion(f32[1,32,25,1024]{3,1,2,0:T(8,128)} %get-tuple-element.25, f32[1,32,25,1024]{3,1,2,0:T(8,128)} %get-tuple-element.24, f32[25,32,1024]{2,0,1:T(8,128)} %fusion.130, ...), kind=kOutput, calls=%fused_computation.97 | convolution fusion | flops 483338816 | bytes 39059456 | tf_op jit(solution)/shard_map/kmc,mj->kjc/dot_general | solution.py:49
  465.4 34.5 %fusion.1 = f32[48,1024,32]{1,2,0:T(8,128)} fusion(f32[32,48]{0,1:T(8,128)S(1)} %fusion.151, f32[32,48]{0,1:T(8,128)S(1)} %get-tuple-element.34, f32[48,32,1024]{2,0,1:T(8,128)S(1)} %fusion.102, f32[48,32,1024]{2,0,1:T(8,128)S(1)} %fusion.98, f32[48,32,1024]{2,0,1:T(8,128)S(1)} %fusion.100, f32[48,32,1024]{2,0,1:T(8,128)} %fusion.96), kind=kOutput, calls=%fused_computation.9 | convolution fusion | flops 611858432 | bytes 31469568 | tf_op jit(solution)/shard_map/nk,kmc->cnm/dot_general | solution.py:84
  500.0 37.9 %multiply_bitcast_fusion = f32[1024,32,48]{0,1,2:T(8,128)} fusion(f32[48,1024,32]{1,2,0:T(8,128)} %fusion.1, f32[32,48]{0,1:T(8,128)S(1)} %fusion.151, f32[32,48]{0,1:T(8,128)S(1)} %get-tuple-element.34, f32[48,32,1024]{2,0,1:T(8,128)S(1)} %fusion.102, f32[48,32,1024]{2,0,1:T(8,128)S(1)} %fusion.98, f32[48,32,1024]{2,0,1:T(8,128)} %copy-done.2, ...), kind=kOutput, calls=%fused_computation.26 | convolution fusion | flops 615004160 | bytes 37761024 | tf_op jit(solution)/shard_map/nk,kmc->cnm/dot_general | solution.py:84
  546.9 44.5 %all-to-all-start = ((f32[16,64,768]{2,1,0:T(8,128)}), f32[16,64,768]{2,1,0:T(8,128)}, u32[]{:S(2)}, u32[]{:S(2)}) async-start(f32[16,64,768]{2,1,0:T(8,128)} %bitcast.46), calls=%async_computation | async-start | bytes 6291456 | tf_op jit(solution)/shard_map/all_to_all | solution.py:146
  622.8 29.8 %fusion.10 = f32[32,48,1024]{2,0,1:T(8,128)} fusion(f32[32,48]{0,1:T(8,128)S(1)} %fusion.151, f32[32,48]{0,1:T(8,128)S(1)} %get-tuple-element.34, f32[48,32,1024]{2,0,1:T(8,128)S(1)} %fusion.94, f32[48,32,1024]{2,0,1:T(8,128)S(1)} %fusion.90, f32[48,32,1024]{2,0,1:T(8,128)S(1)} %fusion.92, f32[48,32,1024]{2,0,1:T(8,128)} %fusion.88), kind=kOutput, calls=%fused_computation.19 | convolution fusion | flops 611858432 | bytes 31469568 | tf_op jit(solution)/shard_map/nk,kmc->nmc/dot_general | solution.py:88
  652.6 30.0 %fusion.7 = f32[32,48,1024]{2,0,1:T(8,128)} fusion(f32[32,48]{0,1:T(8,128)S(1)} %fusion.151, f32[32,48]{0,1:T(8,128)S(1)} %get-tuple-element.34, f32[48,32,1024]{2,0,1:T(8,128)S(1)} %fusion.94, f32[48,32,1024]{2,0,1:T(8,128)S(1)} %fusion.90, f32[48,32,1024]{2,0,1:T(8,128)S(1)} %fusion.92, f32[48,32,1024]{2,0,1:T(8,128)} %fusion.88), kind=kOutput, calls=%fused_computation.17 | convolution fusion | flops 611858432 | bytes 31469568 | tf_op jit(solution)/shard_map/nk,kmc->nmc/dot_general | solution.py:88
  (102 shorter events, 135.8 us)
Async XLA Ops:
  7.2 102.1 %all-gather.2.cloned.1.call-start = ((), (), s32[]{:S(2)}) async-start(), calls=%async_computation.1 | async-start | bytes 6684672 | tf_op jit(solution)/shard_map/all_gather | solution.py:110
  7.9 67.0 %collective-permute-start.2 = (f32[768,1024]{1,0:T(8,128)}, f32[768,1024]{1,0:T(8,128)S(1)}, u32[]{:S(2)}, u32[]{:S(2)}) collective-permute-start(f32[768,1024]{1,0:T(8,128)} %param.6), channel_id=1, source_target_pairs={{2,0},{4,2},{6,4},{8,6},{10,8},{12,10},{14,12},{16,14},{18,16},{20... | collective-permute-start | bytes 9437192 | tf_op jit(solution)/shard_map/ppermute | solution.py:14
  10.5 67.3 %collective-permute-start = (f32[768,1024]{1,0:T(8,128)}, f32[768,1024]{1,0:T(8,128)S(1)}, u32[]{:S(2)}, u32[]{:S(2)}) collective-permute-start(f32[768,1024]{1,0:T(8,128)} %param.5), channel_id=1, source_target_pairs={{0,2},{2,4},{4,6},{6,8},{8,10},{10,12},{12,14},{14,16},{16,18},{18... | collective-permute-start | bytes 9437192 | tf_op jit(solution)/shard_map/ppermute | solution.py:14
  15.2 62.6 %copy-start.7 = (f32[768,1024]{1,0:T(8,128)S(1)}, f32[768,1024]{1,0:T(8,128)}, u32[]{:S(2)}) copy-start(f32[768,1024]{1,0:T(8,128)} %param.5) | copy-start | bytes 9437188
  77.7 21.3 %copy-start = (f32[1536,1024]{1,0:T(8,128)}, f32[1536,1024]{1,0:T(8,128)S(1)}, u32[]{:S(2)}) copy-start(f32[1536,1024]{1,0:T(8,128)S(1)} %pad_maximum_fusion.3) | copy-start | bytes 18874372
  99.0 10.3 %copy-start.8 = (f32[1024]{0:T(1024)S(1)}, f32[1024]{0:T(1024)}, u32[]{:S(2)}) copy-start(f32[1024]{0:T(1024)} %param.8) | copy-start | bytes 12292
  99.0 10.3 %copy-start.9 = (pred[1536]{0:T(1024)(128)(4,1)S(1)}, pred[1536]{0:T(1024)(128)(4,1)}, u32[]{:S(2)}) copy-start(pred[1536]{0:T(1024)(128)(4,1)} %constant.109.clone.1) | copy-start | bytes 4612
  195.9 10.7 %copy-start.1 = (f32[32,48,1024]{2,0,1:T(8,128)S(1)}, f32[32,48,1024]{2,0,1:T(8,128)}, u32[]{:S(2)}) copy-start(f32[32,48,1024]{2,0,1:T(8,128)} %get-tuple-element.13) | copy-start | bytes 18874372
  195.9 19.0 %slice-start.8 = ((s8[6291456]{0:T(1024)(128)(4,1)}), s8[4194304]{0:T(1024)(128)(4,1)S(1)}, s32[]{:S(2)}) async-start(s8[6291456]{0:T(1024)(128)(4,1)} %bitcast.305), calls=%async_computation.10 | async-start | bytes 8388608
  206.7 8.3 %slice-start.9 = ((s8[6291456]{0:T(1024)(128)(4,1)}), s8[2097152]{0:T(1024)(128)(4,1)S(1)}, s32[]{:S(2)}) async-start(s8[6291456]{0:T(1024)(128)(4,1)} %bitcast.305), calls=%async_computation.11 | async-start | bytes 4194304
  214.9 16.7 %slice-start.2 = ((s8[6291456]{0:T(1024)(128)(4,1)}), s8[4194304]{0:T(1024)(128)(4,1)S(1)}, s32[]{:S(2)}) async-start(s8[6291456]{0:T(1024)(128)(4,1)} %bitcast.297), calls=%async_computation.4 | async-start | bytes 8388608
  223.5 8.1 %slice-start.3 = ((s8[6291456]{0:T(1024)(128)(4,1)}), s8[2097152]{0:T(1024)(128)(4,1)S(1)}, s32[]{:S(2)}) async-start(s8[6291456]{0:T(1024)(128)(4,1)} %bitcast.297), calls=%async_computation.5 | async-start | bytes 4194304
  231.6 8.4 %copy-start.6 = (f32[25,32,1024]{2,0,1:T(8,128)S(1)}, f32[25,32,1024]{2,0,1:T(8,128)}, u32[]{:S(2)}) copy-start(f32[25,32,1024]{2,0,1:T(8,128)} %fusion.14) | copy-start | bytes 9830404
  240.1 50.4 %slice-start = ((s8[6291456]{0:T(1024)(128)(4,1)}), s8[4194304]{0:T(1024)(128)(4,1)S(1)}, s32[]{:S(2)}) async-start(s8[6291456]{0:T(1024)(128)(4,1)} %bitcast.295), calls=%async_computation.2 | async-start | bytes 8388608
  248.2 4.7 copy-start.3
  248.2 42.3 %slice-start.1 = ((s8[6291456]{0:T(1024)(128)(4,1)}), s8[2097152]{0:T(1024)(128)(4,1)S(1)}, s32[]{:S(2)}) async-start(s8[6291456]{0:T(1024)(128)(4,1)} %bitcast.295), calls=%async_computation.3 | async-start | bytes 4194304
  252.9 37.6 %copy-start.5 = (f32[25,32,1024]{2,0,1:T(8,128)S(1)}, f32[25,32,1024]{2,0,1:T(8,128)}, u32[]{:S(2)}) copy-start(f32[25,32,1024]{2,0,1:T(8,128)} %fusion.38) | copy-start | bytes 9830404
  263.1 132.7 %collective-permute-start.3 = (f32[2,32,25,1024]{3,1,2,0:T(8,128)}, f32[2,32,25,1024]{3,1,2,0:T(8,128)}, u32[]{:S(2)}, u32[]{:S(2)}) collective-permute-start(f32[2,32,25,1024]{3,1,2,0:T(8,128)} %copy.136), channel_id=1, source_target_pairs={{2,0},{4,2},{6,4},{8,6},{10,8},{12,10},{14,12},{16,14},{18,16},{20... | collective-permute-start | bytes 19660808 | tf_op jit(solution)/shard_map/ppermute | solution.py:14
  298.6 8.8 %copy-start.4 = (f32[25,32,1024]{2,0,1:T(8,128)}, f32[25,32,1024]{2,0,1:T(8,128)S(1)}, u32[]{:S(2)}) copy-start(f32[25,32,1024]{2,0,1:T(8,128)S(1)} %fusion.121) | copy-start | bytes 9830404
  298.7 28.0 %slice-start.6 = ((s8[6291456]{0:T(1024)(128)(4,1)}), s8[2097152]{0:T(1024)(128)(4,1)S(1)}, s32[]{:S(2)}) async-start(s8[6291456]{0:T(1024)(128)(4,1)} %bitcast.301), calls=%async_computation.8 | async-start | bytes 4194304
  307.4 19.2 %slice-start.7 = ((s8[6291456]{0:T(1024)(128)(4,1)}), s8[4194304]{0:T(1024)(128)(4,1)S(1)}, s32[]{:S(2)}) async-start(s8[6291456]{0:T(1024)(128)(4,1)} %bitcast.301), calls=%async_computation.9 | async-start | bytes 8388608
  324.4 78.5 %collective-permute-start.1 = (f32[2,32,25,1024]{3,1,2,0:T(8,128)}, f32[2,32,25,1024]{3,1,2,0:T(8,128)}, u32[]{:S(2)}, u32[]{:S(2)}) collective-permute-start(f32[2,32,25,1024]{3,1,2,0:T(8,128)} %copy.120), channel_id=1, source_target_pairs={{0,2},{2,4},{4,6},{6,8},{8,10},{10,12},{12,14},{14,16},{16,18},{18... | collective-permute-start | bytes 19660808 | tf_op jit(solution)/shard_map/ppermute | solution.py:14
  326.7 16.5 %slice-start.4 = ((s8[6291456]{0:T(1024)(128)(4,1)}), s8[4194304]{0:T(1024)(128)(4,1)S(1)}, s32[]{:S(2)}) async-start(s8[6291456]{0:T(1024)(128)(4,1)} %bitcast.299), calls=%async_computation.6 | async-start | bytes 8388608
  334.7 8.5 %slice-start.5 = ((s8[6291456]{0:T(1024)(128)(4,1)}), s8[2097152]{0:T(1024)(128)(4,1)S(1)}, s32[]{:S(2)}) async-start(s8[6291456]{0:T(1024)(128)(4,1)} %bitcast.299), calls=%async_computation.7 | async-start | bytes 4194304
  343.2 16.6 %slice-start.14 = ((s8[6291456]{0:T(1024)(128)(4,1)}), s8[4194304]{0:T(1024)(128)(4,1)S(1)}, s32[]{:S(2)}) async-start(s8[6291456]{0:T(1024)(128)(4,1)} %bitcast.311), calls=%async_computation.16 | async-start | bytes 8388608
  351.3 8.5 %slice-start.15 = ((s8[6291456]{0:T(1024)(128)(4,1)}), s8[2097152]{0:T(1024)(128)(4,1)S(1)}, s32[]{:S(2)}) async-start(s8[6291456]{0:T(1024)(128)(4,1)} %bitcast.311), calls=%async_computation.17 | async-start | bytes 4194304
  351.3 16.9 %slice-start.10 = ((s8[6291456]{0:T(1024)(128)(4,1)}), s8[2097152]{0:T(1024)(128)(4,1)S(1)}, s32[]{:S(2)}) async-start(s8[6291456]{0:T(1024)(128)(4,1)} %bitcast.307), calls=%async_computation.12 | async-start | bytes 4194304
  359.8 8.4 %slice-start.11 = ((s8[6291456]{0:T(1024)(128)(4,1)}), s8[4194304]{0:T(1024)(128)(4,1)S(1)}, s32[]{:S(2)}) async-start(s8[6291456]{0:T(1024)(128)(4,1)} %bitcast.307), calls=%async_computation.13 | async-start | bytes 8388608
  395.9 14.1 %slice-start.12 = ((s8[6291456]{0:T(1024)(128)(4,1)}), s8[4194304]{0:T(1024)(128)(4,1)S(1)}, s32[]{:S(2)}) async-start(s8[6291456]{0:T(1024)(128)(4,1)} %bitcast.309), calls=%async_computation.14 | async-start | bytes 8388608
  402.9 7.1 %slice-start.13 = ((s8[6291456]{0:T(1024)(128)(4,1)}), s8[2097152]{0:T(1024)(128)(4,1)S(1)}, s32[]{:S(2)}) async-start(s8[6291456]{0:T(1024)(128)(4,1)} %bitcast.309), calls=%async_computation.15 | async-start | bytes 4194304
  458.1 7.3 %copy-start.2 = (f32[48,32,1024]{2,0,1:T(8,128)}, f32[48,32,1024]{2,0,1:T(8,128)S(1)}, u32[]{:S(2)}) copy-start(f32[48,32,1024]{2,0,1:T(8,128)S(1)} %fusion.100) | copy-start | bytes 18874372
  546.9 143.2 %all-to-all-start = ((f32[16,64,768]{2,1,0:T(8,128)}), f32[16,64,768]{2,1,0:T(8,128)}, u32[]{:S(2)}, u32[]{:S(2)}) async-start(f32[16,64,768]{2,1,0:T(8,128)} %bitcast.46), calls=%async_computation | async-start | bytes 6291456 | tf_op jit(solution)/shard_map/all_to_all | solution.py:146
Sparse Core Ops, SparseCore 0:
  10.3 87.6 all-gather.1
where the time goes:
time: 710 us; the launch traced here: 701 us
  matrix products  455 us (64%)
  starting transfers between devices  80.5 us (11%)
  waiting for transfers between devices  60.4 us (9%)
  local copies, waits for them, and re-layouts  52.3 us (7%)
  other arithmetic  38.3 us (5%)
  between operations  15 us (2%)
    dot_general x4, matrix products, forward_real(): jnp.einsum('kn,nmc->kmc', sin_first, grid_view, precision=PRECISE)  70.7 us
    dot_general x4, matrix products, forward_real(): jnp.einsum('kmc,mj->kjc', rot_real, cos_second, precision=PRECISE)  60.1 us
    ppermute x4, waiting for transfers between devices, passed_along(): lax.ppermute(value, axis, [(source, source + steps) for source in range(i...  59.7 us
    all_to_all x1, starting transfers between devices, local(): lax.all_to_all(local_grad, 'ctx', split_axis=0, concat_axis=1, tiled=True)  44.5 us
    dot_general x4, matrix products, forward_real(): jnp.einsum('kn,nmc->kmc', cos_first, grid_view, precision=PRECISE)  41.1 us
    dot_general x1, matrix products, inverse_real(): jnp.einsum('nk,kmc->cnm', sin_first, rot_imag, precision=PRECISE)  37.9 us
    ppermute x4, starting transfers between devices, passed_along(): lax.ppermute(value, axis, [(source, source + steps) for source in range(i...  35.9 us
    dot_general x4, matrix products, forward_real(): jnp.einsum('kmc,mj->kjc', rot_imag, cos_second, precision=PRECISE)  34.9 us
  transfers between devices with their start and end apart: 6, of which 1 were waited for; matrix products, arithmetic and copies ran while one was open for 35% of the time, Pallas kernels for 0%

commit v1 on v0

v1 whole, which is shorter than its diff:
```python
import functools

import jax
import jax.numpy as jnp
import numpy as np
from jax import lax
from jax.experimental import pallas as pl
from jax.experimental.pallas import tpu as pltpu
from jax.sharding import PartitionSpec as P

SUB = 256
LEN = 2 * SUB
JCHUNK = 4


def stacked_halves(table):
    table = table.astype(np.float32)
    high = table.astype(jnp.bfloat16)
    low = (table - high.astype(np.float32)).astype(jnp.bfloat16)
    return np.concatenate([high, high, low], axis=0)


def transform_tables():
    time = np.arange(SUB)
    bins = np.arange(SUB)
    angle = 2.0 * np.pi * (time[:, None] * bins[None, :] % LEN) / LEN
    alternate = np.where(time % 2 == 0, 1.0, -1.0)
    real, imag = np.cos(angle), -np.sin(angle)
    imag[:, 0] = alternate
    forward = np.concatenate([real, imag], axis=1)
    back_real = 2.0 * np.cos(angle.T)
    back_real[0] = 1.0
    back_imag = -2.0 * np.sin(angle.T)
    back_imag[0] = alternate
    inverse = np.concatenate([back_real, back_imag], axis=0) / LEN
    return stacked_halves(forward), stacked_halves(inverse)


def precise_dot(value, table):
    high = value.astype(jnp.bfloat16)
    low = (value - high.astype(jnp.float32)).astype(jnp.bfloat16)
    return jnp.dot(
        jnp.concatenate([high, low, high], axis=1), table, preferred_element_type=jnp.float32
    )


def conv_kernel(adjoint, n, thirds, parts, x_ref, h_ref, d_ref, i_ref, o_ref, w_ref, s_ref, t_ref):
    group = h_ref.shape[0]
    halo = w_ref.shape[1] - n
    base = 0 if adjoint else halo
    lane = lax.broadcasted_iota(jnp.int32, (1, LEN), 1)
    sigma = jnp.where(lane % 2 == 0, 1.0, -1.0).astype(jnp.float32)
    first = lane[:, :SUB] == 0

    taps = jnp.concatenate([h_ref[:, p * SUB : (p + 1) * SUB] for p in range(parts)], axis=0)
    spec = precise_dot(taps, d_ref[...])
    real, imag = spec[:, :SUB], spec[:, SUB:]
    cross = jnp.where(first, 0.0, imag)
    t_ref[0] = real.reshape(parts, group, SUB)
    t_ref[1] = (-cross if adjoint else cross).reshape(parts, group, SUB)
    t_ref[2] = jnp.where(first, imag, real).reshape(parts, group, SUB)

    for t in range(thirds):
        rows = x_ref[:, :, t * SUB : (t + 1) * SUB].reshape(n * group, SUB)
        s_ref[t] = precise_dot(rows, d_ref[...]).reshape(n, group, LEN)

    pad_at = n if adjoint else 0
    w_ref[:, pad_at : pad_at + halo] = jnp.zeros((thirds, halo, group, LEN), jnp.float32)
    for t in range(thirds):
        if adjoint and t == thirds - 1:
            w_ref[t, n - 1] = s_ref[t, n - 1]
            w_ref[t, 0 : n - 1] = s_ref[t, 0 : n - 1] + sigma * s_ref[0, 1:n]
        elif adjoint:
            w_ref[t, 0:n] = s_ref[t] + sigma * s_ref[t + 1]
        elif t == 0:
            w_ref[0, base] = s_ref[0, 0]
            w_ref[0, base + 1 : base + n] = s_ref[0, 1:n] + sigma * s_ref[thirds - 1, 0 : n - 1]
        else:
            w_ref[t, base : base + n] = s_ref[t] + sigma * s_ref[t - 1]

    steps = n // JCHUNK

    def products(index, carry):
        rows = pl.ds(pl.multiple_of(index // steps * 8, 8), 8)
        start = index % steps * JCHUNK
        for t in range(thirds):
            acc_real = acc_imag = 0.0
            for p in range(parts):
                shift, third = divmod(t + p if adjoint else t - p, thirds)
                window = w_ref[third, pl.ds(start + base + shift, JCHUNK), rows, :]
                win_real, win_imag = window[..., :SUB], window[..., SUB:]
                tap_real, tap_cross, tap_last = (t_ref[i, p, rows, :] for i in range(3))
                acc_real += tap_real * win_real - tap_cross * win_imag
                acc_imag += tap_last * win_imag + tap_cross * win_real
            s_ref[t, pl.ds(start, JCHUNK), rows, :SUB] = acc_real
            s_ref[t, pl.ds(start, JCHUNK), rows, SUB:] = acc_imag
        return carry

    lax.fori_loop(0, steps * (group // 8), products, 0)

    for t in range(thirds):
        result = precise_dot(s_ref[t].reshape(n * group, LEN), i_ref[...])
        result = result.reshape(n, group, SUB)
        if adjoint:
            for j in range(n):
                at = (j * thirds + t) * SUB
                o_ref[:, at : at + SUB] = result[j]
        else:
            o_ref[:, :, t * SUB : (t + 1) * SUB] = result


def banded(signal, taps, tables, adjoint):
    n, channels, block = signal.shape
    thirds, parts = block // SUB, taps.shape[1] // SUB
    group = min(32, channels)
    halo = (thirds + parts - 2) // thirds
    if adjoint:
        out_shape = (channels, n * block)
        out_spec = pl.BlockSpec((group, n * block), lambda g: (g, 0))
    else:
        out_shape = (n, channels, block)
        out_spec = pl.BlockSpec((n, group, block), lambda g: (0, g, 0))
    whole = [pl.BlockSpec(table.shape, lambda g: (0, 0)) for table in tables]
    return pl.pallas_call(
        functools.partial(conv_kernel, adjoint, n, thirds, parts),
        out_shape=jax.ShapeDtypeStruct(out_shape, jnp.float32),
        grid=(channels // group,),
        in_specs=[
            pl.BlockSpec((n, group, block), lambda g: (0, g, 0)),
            pl.BlockSpec((group, taps.shape[1]), lambda g: (g, 0)),
            *whole,
        ],
        out_specs=out_spec,
        scratch_shapes=[
            pltpu.VMEM((thirds, n + halo, group, LEN), jnp.float32),
            pltpu.VMEM((thirds, n, group, LEN), jnp.float32),
            pltpu.VMEM((3, parts, group, SUB), jnp.float32),
        ],
        compiler_params=pltpu.CompilerParams(vmem_limit_bytes=48 * 1024 * 1024),
        cost_estimate=pl.CostEstimate(
            flops=12 * signal.size * LEN, bytes_accessed=8 * signal.size, transcendentals=0
        ),
    )(signal, taps, *tables)


def by_owner(value, n):
    rows = value.T.reshape(n, value.shape[1] // n, value.shape[0])
    return lax.all_to_all(rows, "ctx", split_axis=0, concat_axis=0, tiled=True)


def local(inputs, cotangent, filter_rows, skip_gain, band_blocks):
    n = lax.axis_size("ctx")
    block = inputs.shape[0]
    own = inputs.shape[1] // n
    start = lax.axis_index("ctx") * own
    gain = lax.dynamic_slice_in_dim(skip_gain, start, own)
    bands = lax.dynamic_slice_in_dim(band_blocks, start, own)
    tables = tuple(jnp.asarray(table) for table in transform_tables())

    taps = by_owner(filter_rows, n).transpose(1, 0, 2).reshape(own, -1)
    lag = jnp.arange(taps.shape[1], dtype=jnp.int32)[None, :]
    taps = jnp.where(lag < bands[:, None] * block, taps, 0.0)
    taps = taps + jnp.where(lag == 0, gain[:, None], 0.0)

    outputs = banded(by_owner(inputs, n), taps, tables, False)
    outputs = lax.all_to_all(outputs, "ctx", split_axis=0, concat_axis=0, tiled=True)
    outputs = outputs.reshape(n * own, block).T
    input_grad = banded(by_owner(cotangent, n), taps, tables, True)
    return outputs, input_grad


def solution(mesh):
    return jax.shard_map(
        local,
        mesh=mesh,
        in_specs=(P("ctx", "ch"), P("ctx", "ch"), P("ctx", "ch"), P("ch"), P("ch")),
        out_specs=(P("ctx", "ch"), P(("ch", "ctx"), None)),
        check_vma=False,
    )
```

time: 710 us -> 253 us (0.36); the launches traced: 701 us -> 252 us
  matrix products: 455 us -> 0 us
  waiting for transfers between devices: 60.4 us -> 175 us
  starting transfers between devices: 80.5 us -> 21.4 us
  other arithmetic: 38.3 us -> 1.92 us
  Pallas kernels: 0 us -> 29.1 us
  local copies, waits for them, and re-layouts: 52.3 us -> 23.3 us
  between operations: 15 us -> 0.68 us
    dot_general x36 -> x0, matrix products: 455 us -> none  [the longest x4 70.7 us: forward_real(): jnp.einsum('kn,nmc->kmc', sin_first, grid_view, precision=PRECISE)]
    all_to_all x1 -> x4, waiting for transfers between devices: 0.01 us -> 175 us  [the longest x3 122 us: by_owner(): return lax.all_to_all(rows, 'ctx', split_axis=0, concat_axis=0, tiled=True)]
    ppermute x4 -> x0, waiting for transfers between devices: 59.7 us -> none  [passed_along(): lax.ppermute(value, axis, [(source, source + steps) for source in range(i...]
    ppermute x4 -> x0, starting transfers between devices: 35.9 us -> none  [passed_along(): lax.ppermute(value, axis, [(source, source + steps) for source in range(i...]
    pallas_call x0 -> x2, Pallas kernels: none -> 29.1 us  [banded(): pl.pallas_call(functools.partial(conv_kernel, adjoint, n, thirds, parts),...]
    all_to_all x1 -> x4, starting transfers between devices: 44.5 us -> 21.4 us  [the longest x3 16.6 us: by_owner(): return lax.all_to_all(rows, 'ctx', split_axis=0, concat_axis=0, tiled=True)]
    slice x6 -> x0, local copies, waits for them, and re-layouts: 20.5 us -> none  [the longest x2 14 us: spectral_product(): panel_real, panel_imag = (panel_spec[0], panel_spec[1])]
    another operation x2 -> x0, local copies, waits for them, and re-layouts: 20.2 us -> none  [forward_real(): return jnp.stack([out_real, out_imag])]
  transfers between devices with their start and end apart: 6 -> 4, of which waited for: 1 -> 4; matrix products, arithmetic and copies ran while one was open for 35% -> 5% of each run, Pallas kernels for 0% -> 12%
where the time goes in v1:
time: 253 us; the launch traced here: 252 us
  waiting for transfers between devices  175 us (69%)
  Pallas kernels  29.1 us (12%)
  local copies, waits for them, and re-layouts  23.3 us (9%)
  starting transfers between devices  21.4 us (8%)
    all_to_all x3, waiting for transfers between devices, by_owner(): return lax.all_to_all(rows, 'ctx', split_axis=0, concat_axis=0, tiled=True)  122 us
    all_to_all x1, waiting for transfers between devices, local(): lax.all_to_all(outputs, 'ctx', split_axis=0, concat_axis=0, tiled=True)  53.3 us
    pallas_call x2, Pallas kernels, banded(): pl.pallas_call(functools.partial(conv_kernel, adjoint, n, thirds, parts),...  29.1 us
    all_to_all x3, starting transfers between devices, by_owner(): return lax.all_to_all(rows, 'ctx', split_axis=0, concat_axis=0, tiled=True)  16.6 us
    unnamed x15, local copies, waits for them, and re-layouts  8.97 us
    transpose x2, local copies, waits for them, and re-layouts, by_owner(): rows = value.T.reshape(n, value.shape[1] // n, value.shape[0])  5.91 us
  transfers between devices with their start and end apart: 4, of which 4 were waited for; matrix products, arithmetic and copies ran while one was open for 5% of the time, Pallas kernels for 12%

profile of v1, /device:TPU:13, one launch (start us, length us, event | category | flops | bytes accessed | tf_op | source)
XLA Modules:
  0.0 251.8 jit_solution(8904159793415255838)
XLA Ops:
  0.6 2.0 copy.14
  2.6 6.5 %all-to-all-start.1 = ((f32[16,64,96]{2,1,0:T(8,128)}), f32[16,64,96]{2,1,0:T(8,128)S(1)}, u32[]{:S(2)}, u32[]{:S(2)}) async-start(f32[16,64,96]{2,1,0:T(8,128)} %bitcast.3), calls=%async_computation.1 | async-start | bytes 1048576 | tf_op jit(solution)/shard_map/all_to_all | solution.py:148
  9.1 3.5 %copy.13 = f32[1024,768]{1,0:T(8,128)} copy(f32[1024,768]{0,1:T(8,128)} %bitcast.11) | data formatting | bytes 6291456 | tf_op jit(solution)/shard_map/transpose | solution.py:147
  12.7 10.0 %all-to-all-done.1 = f32[16,64,96]{2,1,0:T(8,128)S(1)} async-done(((f32[16,64,96]{2,1,0:T(8,128)}), f32[16,64,96]{2,1,0:T(8,128)S(1)}, u32[]{:S(2)}, u32[]{:S(2)}) %all-to-all-start.1) | async-done | bytes 393248 | tf_op jit(solution)/shard_map/all_to_all | solution.py:148
  22.7 0.0 copy-start.6
  22.7 0.8 copy-done.6
  23.5 0.0 copy-start.5
  23.5 5.3 %all-to-all-start = ((f32[16,64,768]{2,1,0:T(8,128)}), f32[16,64,768]{2,1,0:T(8,128)}, u32[]{:S(2)}, u32[]{:S(2)}) async-start(f32[16,64,768]{2,1,0:T(8,128)} %bitcast.1), calls=%async_computation | async-start | bytes 6291456 | tf_op jit(solution)/shard_map/all_to_all | solution.py:148
  28.8 0.0 copy-done.5
  28.8 2.4 copy.17
  31.2 67.6 %all-to-all-done.x_ref = f32[16,64,768]{2,1,0:T(8,128)} async-done(((f32[16,64,768]{2,1,0:T(8,128)}), f32[16,64,768]{2,1,0:T(8,128)}, u32[]{:S(2)}, u32[]{:S(2)}) %all-to-all-start) | async-done | bytes 3145760 | tf_op jit(solution)/shard_map/all_to_all | solution.py:148
  98.9 4.8 %all-to-all-start.3 = ((f32[16,64,768]{2,1,0:T(8,128)}), f32[16,64,768]{2,1,0:T(8,128)S(1)}, u32[]{:S(2)}, u32[]{:S(2)}) async-start(f32[16,64,768]{2,1,0:T(8,128)} %bitcast.10), calls=%async_computation.3 | async-start | bytes 6291456 | tf_op jit(solution)/shard_map/all_to_all | solution.py:148
  103.6 0.8 dynamic_slice.7
  104.4 0.8 dynamic-slice_multiply_fusion
  105.1 2.1 copy.15
  107.3 2.0 reshape.29
  109.3 1.1 select_add_fusion.h_ref
  110.5 0.0 copy-start.1
  110.5 1.1 copy-done.1
  111.6 1.1 copy-done.3
  112.7 14.7 %shard_map.86 = f32[16,64,768]{2,1,0:T(8,128)S(1)} custom-call(f32[16,64,768]{2,1,0:T(8,128)} %all-to-all-done.x_ref, f32[64,1536]{1,0:T(8,128)S(1)} %select_add_fusion.h_ref, bf16[768,512]{1,0:T(8,128)(2,1)S(1)} %copy-done.3, bf16[1536,256]{1,0:T(8,128)(2,1)S(1)} %copy-done.1), custom_call_target="tpu_custom_call" | custom-call | flops 4831838208 | bytes 6291456 | tf_op jit(solution)/shard_map/pallas_call | solution.py:124
  127.4 0.0 copy-start
  127.4 1.7 copy-done
  129.1 44.4 %all-to-all-done.3.x_ref = f32[16,64,768]{2,1,0:T(8,128)S(1)} async-done(((f32[16,64,768]{2,1,0:T(8,128)}), f32[16,64,768]{2,1,0:T(8,128)S(1)}, u32[]{:S(2)}, u32[]{:S(2)}) %all-to-all-start.3) | async-done | bytes 3145760 | tf_op jit(solution)/shard_map/all_to_all | solution.py:148
  173.5 4.8 %all-to-all-start.2 = ((f32[16,64,768]{2,1,0:T(8,128)}), f32[16,64,768]{2,1,0:T(8,128)}, u32[]{:S(2)}, u32[]{:S(2)}) async-start(f32[16,64,768]{2,1,0:T(8,128)} %copy-done), calls=%async_computation.2 | async-start | bytes 6291456 | tf_op jit(solution)/shard_map/all_to_all | solution.py:166
  178.3 0.0 copy-start.2
  178.3 1.1 copy-done.2
  179.4 0.0 copy-start.4
  179.4 1.1 copy-done.4
  180.6 14.4 %shard_map.87 = f32[64,12288]{1,0:T(8,128)} custom-call(f32[16,64,768]{2,1,0:T(8,128)S(1)} %all-to-all-done.3.x_ref, f32[64,1536]{1,0:T(8,128)S(1)} %select_add_fusion.h_ref, bf16[768,512]{1,0:T(8,128)(2,1)S(1)} %copy-done.4, bf16[1536,256]{1,0:T(8,128)(2,1)S(1)} %copy-done.2), custom_call_target="tpu_custom_call" | custom-call | flops 4831838208 | bytes 6291456 | tf_op jit(solution)/shard_map/pallas_call | solution.py:124
  195.0 53.3 %all-to-all-done.2 = f32[16,64,768]{2,1,0:T(8,128)} async-done(((f32[16,64,768]{2,1,0:T(8,128)}), f32[16,64,768]{2,1,0:T(8,128)}, u32[]{:S(2)}, u32[]{:S(2)}) %all-to-all-start.2) | async-done | bytes 3145760 | tf_op jit(solution)/shard_map/all_to_all | solution.py:166
  248.3 3.5 %copy.16 = f32[1024,768]{0,1:T(8,128)} copy(f32[1024,768]{1,0:T(8,128)} %bitcast.5) | data formatting | bytes 6291456 | tf_op jit(solution)/shard_map/reshape | solution.py:167
  (2 shorter events, 0.0 us)
Async XLA Ops:
  2.6 20.1 %all-to-all-start.1 = ((f32[16,64,96]{2,1,0:T(8,128)}), f32[16,64,96]{2,1,0:T(8,128)S(1)}, u32[]{:S(2)}, u32[]{:S(2)}) async-start(f32[16,64,96]{2,1,0:T(8,128)} %bitcast.3), calls=%async_computation.1 | async-start | bytes 1048576 | tf_op jit(solution)/shard_map/all_to_all | solution.py:148
  22.7 0.8 copy-start.6
  23.5 5.3 %copy-start.5 = (f32[768,1024]{1,0:T(8,128)S(1)}, f32[768,1024]{1,0:T(8,128)}, u32[]{:S(2)}) copy-start(f32[768,1024]{1,0:T(8,128)} %param.8) | copy-start | bytes 9437188
  23.5 75.3 %all-to-all-start = ((f32[16,64,768]{2,1,0:T(8,128)}), f32[16,64,768]{2,1,0:T(8,128)}, u32[]{:S(2)}, u32[]{:S(2)}) async-start(f32[16,64,768]{2,1,0:T(8,128)} %bitcast.1), calls=%async_computation | async-start | bytes 6291456 | tf_op jit(solution)/shard_map/all_to_all | solution.py:148
  98.9 74.6 %all-to-all-start.3 = ((f32[16,64,768]{2,1,0:T(8,128)}), f32[16,64,768]{2,1,0:T(8,128)S(1)}, u32[]{:S(2)}, u32[]{:S(2)}) async-start(f32[16,64,768]{2,1,0:T(8,128)} %bitcast.10), calls=%async_computation.3 | async-start | bytes 6291456 | tf_op jit(solution)/shard_map/all_to_all | solution.py:148
  110.5 1.1 copy-start.1
  111.6 1.1 copy-start.3
  127.4 1.7 copy-start
  173.5 74.8 %all-to-all-start.2 = ((f32[16,64,768]{2,1,0:T(8,128)}), f32[16,64,768]{2,1,0:T(8,128)}, u32[]{:S(2)}, u32[]{:S(2)}) async-start(f32[16,64,768]{2,1,0:T(8,128)} %copy-done), calls=%async_computation.2 | async-start | bytes 6291456 | tf_op jit(solution)/shard_map/all_to_all | solution.py:166
  178.3 1.1 copy-start.2
  179.4 1.1 copy-start.4

commit v2 on v1

--- a/solution.py
+++ b/solution.py
@@ -11,6 +11,8 @@
 SUB = 256
 LEN = 2 * SUB
 JCHUNK = 4
+OUTER = 4
+BOTH = ("outer", "inner")
 
 
 def stacked_halves(table):
@@ -44,8 +46,11 @@
     )
 
 
-def conv_kernel(adjoint, n, thirds, parts, x_ref, h_ref, d_ref, i_ref, o_ref, w_ref, s_ref, t_ref):
+def conv_kernel(adjoint, thirds, parts, *refs):
+    *signals, h_ref, d_ref, i_ref, o_ref, w_ref, s_ref, t_ref = refs
     group = h_ref.shape[0]
+    n = signals[-1].shape[0]
+    total = sum(ref.shape[0] for ref in signals)
     halo = w_ref.shape[1] - n
     base = 0 if adjoint else halo
     lane = lax.broadcasted_iota(jnp.int32, (1, LEN), 1)
@@ -61,11 +66,12 @@
     t_ref[2] = jnp.where(first, imag, real).reshape(parts, group, SUB)
 
     for t in range(thirds):
-        rows = x_ref[:, :, t * SUB : (t + 1) * SUB].reshape(n * group, SUB)
-        s_ref[t] = precise_dot(rows, d_ref[...]).reshape(n, group, LEN)
-
-    pad_at = n if adjoint else 0
-    w_ref[:, pad_at : pad_at + halo] = jnp.zeros((thirds, halo, group, LEN), jnp.float32)
+        rows = [ref[:, :, t * SUB : (t + 1) * SUB].reshape(-1, SUB) for ref in signals]
+        spectra = precise_dot(jnp.concatenate(rows, axis=0), d_ref[...])
+        s_ref[t] = spectra.reshape(total, group, LEN)
+
+    if adjoint:
+        w_ref[:, n : n + halo] = jnp.zeros((thirds, halo, group, LEN), jnp.float32)
     for t in range(thirds):
         if adjoint and t == thirds - 1:
             w_ref[t, n - 1] = s_ref[t, n - 1]
@@ -73,10 +79,10 @@
         elif adjoint:
             w_ref[t, 0:n] = s_ref[t] + sigma * s_ref[t + 1]
         elif t == 0:
-            w_ref[0, base] = s_ref[0, 0]
-            w_ref[0, base + 1 : base + n] = s_ref[0, 1:n] + sigma * s_ref[thirds - 1, 0 : n - 1]
+            w_ref[0, 0] = s_ref[0, 0]
+            w_ref[0, 1:total] = s_ref[0, 1:total] + sigma * s_ref[thirds - 1, 0 : total - 1]
         else:
-            w_ref[t, base : base + n] = s_ref[t] + sigma * s_ref[t - 1]
+            w_ref[t] = s_ref[t] + sigma * s_ref[t - 1]
 
     steps = n // JCHUNK
 
@@ -99,7 +105,7 @@
     lax.fori_loop(0, steps * (group // 8), products, 0)
 
     for t in range(thirds):
-        result = precise_dot(s_ref[t].reshape(n * group, LEN), i_ref[...])
+        result = precise_dot(s_ref[t, 0:n].reshape(n * group, LEN), i_ref[...])
         result = result.reshape(n, group, SUB)
         if adjoint:
             for j in range(n):
@@ -109,50 +115,59 @@
             o_ref[:, :, t * SUB : (t + 1) * SUB] = result
 
 
-def banded(signal, taps, tables, adjoint):
-    n, channels, block = signal.shape
+def banded(signals, taps, tables, adjoint):
+    n, channels, block = signals[-1].shape
     thirds, parts = block // SUB, taps.shape[1] // SUB
     group = min(32, channels)
-    halo = (thirds + parts - 2) // thirds
+    halo = halo_blocks(block, taps)
+    total = sum(signal.shape[0] for signal in signals)
     if adjoint:
         out_shape = (channels, n * block)
         out_spec = pl.BlockSpec((group, n * block), lambda g: (g, 0))
     else:
         out_shape = (n, channels, block)
         out_spec = pl.BlockSpec((n, group, block), lambda g: (0, g, 0))
+    pieces = [
+        pl.BlockSpec((signal.shape[0], group, block), lambda g: (0, g, 0)) for signal in signals
+    ]
     whole = [pl.BlockSpec(table.shape, lambda g: (0, 0)) for table in tables]
     return pl.pallas_call(
-        functools.partial(conv_kernel, adjoint, n, thirds, parts),
+        functools.partial(conv_kernel, adjoint, thirds, parts),
         out_shape=jax.ShapeDtypeStruct(out_shape, jnp.float32),
         grid=(channels // group,),
-        in_specs=[
-            pl.BlockSpec((n, group, block), lambda g: (0, g, 0)),
-            pl.BlockSpec((group, taps.shape[1]), lambda g: (g, 0)),
-            *whole,
-        ],
+        in_specs=[*pieces, pl.BlockSpec((group, taps.shape[1]), lambda g: (g, 0)), *whole],
         out_specs=out_spec,
         scratch_shapes=[
             pltpu.VMEM((thirds, n + halo, group, LEN), jnp.float32),
-            pltpu.VMEM((thirds, n, group, LEN), jnp.float32),
+            pltpu.VMEM((thirds, total, group, LEN), jnp.float32),
             pltpu.VMEM((3, parts, group, SUB), jnp.float32),
         ],
         compiler_params=pltpu.CompilerParams(vmem_limit_bytes=48 * 1024 * 1024),
         cost_estimate=pl.CostEstimate(
-            flops=12 * signal.size * LEN, bytes_accessed=8 * signal.size, transcendentals=0
+            flops=12 * n * channels * block * LEN,
+            bytes_accessed=8 * n * channels * block,
+            transcendentals=0,
         ),
-    )(signal, taps, *tables)
+    )(*signals, taps, *tables)
+
+
+def halo_blocks(block, taps):
+    thirds, parts = block // SUB, taps.shape[1] // SUB
+    return (thirds + parts - 2) // thirds
 
 
 def by_owner(value, n):
     rows = value.T.reshape(n, value.shape[1] // n, value.shape[0])
-    return lax.all_to_all(rows, "ctx", split_axis=0, concat_axis=0, tiled=True)
+    return lax.all_to_all(rows, BOTH, split_axis=0, concat_axis=0, tiled=True)
 
 
 def local(inputs, cotangent, filter_rows, skip_gain, band_blocks):
-    n = lax.axis_size("ctx")
+    outer, inner = lax.axis_size("outer"), lax.axis_size("inner")
+    outer_at = lax.axis_index("outer")
+    n = outer * inner
     block = inputs.shape[0]
     own = inputs.shape[1] // n
-    start = lax.axis_index("ctx") * own
+    start = (outer_at * inner + lax.axis_index("inner")) * own
     gain = lax.dynamic_slice_in_dim(skip_gain, start, own)
     bands = lax.dynamic_slice_in_dim(band_blocks, start, own)
     tables = tuple(jnp.asarray(table) for table in transform_tables())
@@ -161,19 +176,36 @@
     lag = jnp.arange(taps.shape[1], dtype=jnp.int32)[None, :]
     taps = jnp.where(lag < bands[:, None] * block, taps, 0.0)
     taps = taps + jnp.where(lag == 0, gain[:, None], 0.0)
-
-    outputs = banded(by_owner(inputs, n), taps, tables, False)
-    outputs = lax.all_to_all(outputs, "ctx", split_axis=0, concat_axis=0, tiled=True)
-    outputs = outputs.reshape(n * own, block).T
-    input_grad = banded(by_owner(cotangent, n), taps, tables, True)
+    column_taps = jnp.zeros((outer * own, taps.shape[1]), jnp.float32)
+    for step in range(outer):
+        piece = taps
+        if step:
+            ring = [(i, (i + step) % outer) for i in range(outer)]
+            piece = lax.ppermute(taps, "outer", ring)
+        row = (outer_at - step) % outer * own
+        column_taps = lax.dynamic_update_slice(column_taps, piece, (row, 0))
+
+    rows = inputs.T.reshape(outer, inner, own, block).transpose(1, 0, 2, 3)
+    rows = rows.reshape(inner, outer * own, block)
+    rows = lax.all_to_all(rows, "inner", split_axis=0, concat_axis=0, tiled=True)
+    halo = halo_blocks(block, taps)
+    before = lax.ppermute(rows[inner - halo :], "outer", [(i, i + 1) for i in range(outer - 1)])
+    outputs = banded((before, rows), column_taps, tables, False)
+    outputs = lax.all_to_all(outputs, "inner", split_axis=0, concat_axis=0, tiled=True)
+    outputs = outputs.reshape(inner, outer, own, block).transpose(3, 1, 0, 2)
+    outputs = outputs.reshape(block, n * own)
+
+    input_grad = banded((by_owner(cotangent, n),), taps, tables, True)
     return outputs, input_grad
 
 
 def solution(mesh):
+    devices = mesh.devices
+    devices = devices.reshape(OUTER, devices.shape[0] // OUTER, devices.shape[1])
     return jax.shard_map(
         local,
-        mesh=mesh,
-        in_specs=(P("ctx", "ch"), P("ctx", "ch"), P("ctx", "ch"), P("ch"), P("ch")),
-        out_specs=(P("ctx", "ch"), P(("ch", "ctx"), None)),
+        mesh=jax.sharding.Mesh(devices, ("outer", "inner", "ch")),
+        in_specs=(P(BOTH, "ch"), P(BOTH, "ch"), P(BOTH, "ch"), P("ch"), P("ch")),
+        out_specs=(P(BOTH, "ch"), P(("ch", "outer", "inner"), None)),
         check_vma=False,
     )

time: 253 us -> 275 us (1.087)
  local copies, waits for them, and re-layouts: 23.3 us -> 31.7 us
  starting transfers between devices: 21.4 us -> 28.7 us
  Pallas kernels: 29.1 us -> 33.6 us
    ppermute x0 -> x4, waiting for transfers between devices: none -> 116 us  [the longest x3 116 us: local(): piece = lax.ppermute(taps, 'outer', ring)]
    all_to_all x4, waiting for transfers between devices: 175 us -> 59.7 us  [the longest x1 31.9 us: local(): lax.all_to_all(rows, 'inner', split_axis=0, concat_axis=0, tiled=True)]
    ppermute x0 -> x4, starting transfers between devices: none -> 6.7 us  [the longest x3 3.49 us: local(): piece = lax.ppermute(taps, 'outer', ring)]
    pallas_call x2, Pallas kernels: 29.1 us -> 33.6 us  [banded(): pl.pallas_call(functools.partial(conv_kernel, adjoint, thirds, parts), ou...]
    dynamic_update_slice x0 -> x3, local copies, waits for them, and re-layouts: none -> 4.35 us  [local(): column_taps = lax.dynamic_update_slice(column_taps, piece, (row, 0))]
    transpose x2 -> x1, local copies, waits for them, and re-layouts: 5.91 us -> 3.53 us  [by_owner(): rows = value.T.reshape(n, value.shape[1] // n, value.shape[0])]
  transfers between devices with their start and end apart: 4 -> 8, of which waited for: 4 -> 5; matrix products, arithmetic and copies ran while one was open for 5% -> 8% of each run, Pallas kernels for 12% -> 12%
where the time goes in v2:
time: 275 us; the launch traced here: 272 us
  waiting for transfers between devices  176 us (64%)
  Pallas kernels  33.6 us (12%)
  local copies, waits for them, and re-layouts  31.7 us (12%)
  starting transfers between devices  28.7 us (10%)
    ppermute x3, waiting for transfers between devices, local(): piece = lax.ppermute(taps, 'outer', ring)  116 us
    pallas_call x2, Pallas kernels, banded(): pl.pallas_call(functools.partial(conv_kernel, adjoint, thirds, parts), ou...  33.6 us
    all_to_all x1, waiting for transfers between devices, local(): lax.all_to_all(rows, 'inner', split_axis=0, concat_axis=0, tiled=True)  31.9 us
    all_to_all x1, waiting for transfers between devices, local(): lax.all_to_all(outputs, 'inner', split_axis=0, concat_axis=0, tiled=True)  18.4 us
    all_to_all x2, starting transfers between devices, by_owner(): return lax.all_to_all(rows, BOTH, split_axis=0, concat_axis=0, tiled=True)  12 us
    unnamed x15, local copies, waits for them, and re-layouts  10.7 us
    all_to_all x2, waiting for transfers between devices, by_owner(): return lax.all_to_all(rows, BOTH, split_axis=0, concat_axis=0, tiled=True)  9.33 us
    all_to_all x1, starting transfers between devices, local(): lax.all_to_all(outputs, 'inner', split_axis=0, concat_axis=0, tiled=True)  5.83 us
  transfers between devices with their start and end apart: 8, of which 5 were waited for; matrix products, arithmetic and copies ran while one was open for 8% of the time, Pallas kernels for 12%

profile of v2, /device:TPU:13, one launch (start us, length us, event | category | flops | bytes accessed | tf_op | source)
XLA Modules:
  0.0 271.9 jit_solution(16305275748897771918)
XLA Ops:
  0.6 2.0 copy.15
  2.6 6.5 %all-to-all-start.1 = ((f32[16,64,96]{2,1,0:T(8,128)}), f32[16,64,96]{2,1,0:T(8,128)}, u32[]{:S(2)}, u32[]{:S(2)}) async-start(f32[16,64,96]{2,1,0:T(8,128)} %bitcast.5), calls=%async_computation.1 | async-start | bytes 1048576 | tf_op jit(solution)/shard_map/all_to_all | solution.py:161
  9.1 2.4 copy.13
  11.5 2.0 copy.14
  13.5 9.3 %all-to-all-done.1 = f32[16,64,96]{2,1,0:T(8,128)} async-done(((f32[16,64,96]{2,1,0:T(8,128)}), f32[16,64,96]{2,1,0:T(8,128)}, u32[]{:S(2)}, u32[]{:S(2)}) %all-to-all-start.1) | async-done | bytes 393248 | tf_op jit(solution)/shard_map/all_to_all | solution.py:161
  22.8 4.2 %all-to-all-start = ((f32[4,256,768]{2,1,0:T(8,128)}), f32[4,256,768]{2,1,0:T(8,128)S(1)}, u32[]{:S(2)}, u32[]{:S(2)}) async-start(f32[4,256,768]{2,1,0:T(8,128)} %bitcast.3), calls=%async_computation | async-start | bytes 6291456 | tf_op jit(solution)/shard_map/all_to_all | solution.py:190
  27.0 3.5 %copy.18 = f32[1024,768]{1,0:T(8,128)} copy(f32[1024,768]{0,1:T(8,128)} %bitcast.19) | data formatting | bytes 6291456 | tf_op jit(solution)/shard_map/transpose | solution.py:160
  30.5 31.9 %all-to-all-done.refs_1_ = f32[4,256,768]{2,1,0:T(8,128)S(1)} async-done(((f32[4,256,768]{2,1,0:T(8,128)}), f32[4,256,768]{2,1,0:T(8,128)S(1)}, u32[]{:S(2)}, u32[]{:S(2)}) %all-to-all-start) | async-done | bytes 3145760 | tf_op jit(solution)/shard_map/all_to_all | solution.py:190
  62.4 1.7 copy-done.4
  64.1 5.5 %all-to-all-start.3 = ((f32[16,64,768]{2,1,0:T(8,128)}), f32[16,64,768]{2,1,0:T(8,128)S(1)}, u32[]{:S(2)}, u32[]{:S(2)}) async-start(f32[16,64,768]{2,1,0:T(8,128)} %bitcast.16), calls=%async_computation.3 | async-start | bytes 6291456 | tf_op jit(solution)/shard_map/all_to_all | solution.py:161
  70.3 0.8 dynamic-slice_multiply_fusion
  71.1 2.1 copy.16
  73.2 2.0 reshape.36
  75.3 2.7 slice.4
  77.9 3.2 %collective-permute-start = (f32[2,256,768]{2,1,0:T(8,128)}, f32[2,256,768]{2,1,0:T(8,128)}, u32[]{:S(2)}, u32[]{:S(2)}) collective-permute-start(f32[2,256,768]{2,1,0:T(8,128)} %slice.4), channel_id=1, source_target_pairs={{0,8},{8,16},{16,24},{1,9},{9,17},{17,25},{2,10},{10,18},{18,26},{... | collective-permute-start | bytes 4718600 | tf_op jit(solution)/shard_map/ppermute | solution.py:192
  81.2 1.4 broadcast_in_dim.28
  82.5 0.9 constant_dynamic-update-slice_fusion.3
  83.5 1.2 collective-permute-start.1
  84.6 2.3 collective-permute-start.2
  87.0 109.2 %collective-permute-done.1 = f32[64,1536]{1,0:T(8,128)} collective-permute-done((f32[64,1536]{1,0:T(8,128)S(1)}, f32[64,1536]{1,0:T(8,128)}, u32[]{:S(2)}, u32[]{:S(2)}) %collective-permute-start.1) | collective-permute-done | bytes 393248 | tf_op jit(solution)/shard_map/ppermute | solution.py:184
  196.2 1.8 constant_dynamic-update-slice_fusion.2
  198.0 6.7 %collective-permute-done.2 = f32[64,1536]{1,0:T(8,128)} collective-permute-done((f32[64,1536]{1,0:T(8,128)S(1)}, f32[64,1536]{1,0:T(8,128)}, u32[]{:S(2)}, u32[]{:S(2)}) %collective-permute-start.2) | collective-permute-done | bytes 393248 | tf_op jit(solution)/shard_map/ppermute | solution.py:184
  204.6 1.8 constant_dynamic-update-slice_fusion.1
  206.4 0.8 constant_dynamic-update-slice_fusion.refs_2_
  207.2 19.1 %shard_map.86 = f32[4,256,768]{2,1,0:T(8,128)} custom-call(f32[2,256,768]{2,1,0:T(8,128)} %collective-permute-done.refs_0_, f32[4,256,768]{2,1,0:T(8,128)} %copy-done.4, f32[256,1536]{1,0:T(8,128)} %constant_dynamic-update-slice_fusion.refs_2_, bf16[768,512]{1,0:T(8,128)(2,1)S(1)} %copy-done.2, bf16[1536,256]{1,0:T(8,128)(2,1)S(1)} %copy-done), custom_call_target="tpu_custom_call" | custom-call | flops 4831838208 | bytes 6291456 | tf_op jit(solution)/shard_map/pallas_call | solution.py:134
  226.4 5.8 %all-to-all-start.2 = ((f32[4,256,768]{2,1,0:T(8,128)}), f32[4,256,768]{2,1,0:T(8,128)}, u32[]{:S(2)}, u32[]{:S(2)}) async-start(f32[4,256,768]{2,1,0:T(8,128)} %shard_map.86), calls=%async_computation.2 | async-start | bytes 6291456 | tf_op jit(solution)/shard_map/all_to_all | solution.py:194
  232.2 1.1 copy-done.1
  233.3 1.1 copy-done.3
  234.5 14.4 %shard_map.87 = f32[64,12288]{1,0:T(8,128)} custom-call(f32[16,64,768]{2,1,0:T(8,128)S(1)} %all-to-all-done.3.refs_0_, f32[64,1536]{1,0:T(8,128)S(1)} %get-tuple-element.5.refs_1_, bf16[768,512]{1,0:T(8,128)(2,1)S(1)} %copy-done.3, bf16[1536,256]{1,0:T(8,128)(2,1)S(1)} %copy-done.1), custom_call_target="tpu_custom_call" | custom-call | flops 4831838208 | bytes 6291456 | tf_op jit(solution)/shard_map/pallas_call | solution.py:134
  248.9 18.4 %all-to-all-done.2 = f32[4,256,768]{2,1,0:T(8,128)} async-done(((f32[4,256,768]{2,1,0:T(8,128)}), f32[4,256,768]{2,1,0:T(8,128)}, u32[]{:S(2)}, u32[]{:S(2)}) %all-to-all-start.2) | async-done | bytes 3145760 | tf_op jit(solution)/shard_map/all_to_all | solution.py:194
  267.3 2.2 copy.17
  269.5 2.4 copy.19
  (15 shorter events, 0.8 us)
Async XLA Ops:
  2.6 20.2 %all-to-all-start.1 = ((f32[16,64,96]{2,1,0:T(8,128)}), f32[16,64,96]{2,1,0:T(8,128)}, u32[]{:S(2)}, u32[]{:S(2)}) async-start(f32[16,64,96]{2,1,0:T(8,128)} %bitcast.5), calls=%async_computation.1 | async-start | bytes 1048576 | tf_op jit(solution)/shard_map/all_to_all | solution.py:161
  22.8 39.6 %all-to-all-start = ((f32[4,256,768]{2,1,0:T(8,128)}), f32[4,256,768]{2,1,0:T(8,128)S(1)}, u32[]{:S(2)}, u32[]{:S(2)}) async-start(f32[4,256,768]{2,1,0:T(8,128)} %bitcast.3), calls=%async_computation | async-start | bytes 6291456 | tf_op jit(solution)/shard_map/all_to_all | solution.py:190
  62.4 1.7 copy-start.4
  64.1 162.3 %all-to-all-start.3 = ((f32[16,64,768]{2,1,0:T(8,128)}), f32[16,64,768]{2,1,0:T(8,128)S(1)}, u32[]{:S(2)}, u32[]{:S(2)}) async-start(f32[16,64,768]{2,1,0:T(8,128)} %bitcast.16), calls=%async_computation.3 | async-start | bytes 6291456 | tf_op jit(solution)/shard_map/all_to_all | solution.py:161
  77.9 4.6 %copy-start.5 = (f32[64,1536]{1,0:T(8,128)S(1)}, f32[64,1536]{1,0:T(8,128)}, u32[]{:S(2)}) copy-start(f32[64,1536]{1,0:T(8,128)} %reshape.36) | copy-start | bytes 1179652
  77.9 129.3 %collective-permute-start = (f32[2,256,768]{2,1,0:T(8,128)}, f32[2,256,768]{2,1,0:T(8,128)}, u32[]{:S(2)}, u32[]{:S(2)}) collective-permute-start(f32[2,256,768]{2,1,0:T(8,128)} %slice.4), channel_id=1, source_target_pairs={{0,8},{8,16},{16,24},{1,9},{9,17},{17,25},{2,10},{10,18},{18,26},{... | collective-permute-start | bytes 4718600 | tf_op jit(solution)/shard_map/ppermute | solution.py:192
  83.5 112.7 %collective-permute-start.1 = (f32[64,1536]{1,0:T(8,128)S(1)}, f32[64,1536]{1,0:T(8,128)}, u32[]{:S(2)}, u32[]{:S(2)}) collective-permute-start(f32[64,1536]{1,0:T(8,128)S(1)} %get-tuple-element.5.refs_1_), channel_id=1, source_target_pairs={{0,8},{8,16},{16,24},{24,0},{1,9},{9,17},{17,25},{25,1},{2,10},{10... | collective-permute-start | bytes 1179656 | tf_op jit(solution)/shard_map/ppermute | solution.py:184
  84.6 120.0 %collective-permute-start.2 = (f32[64,1536]{1,0:T(8,128)S(1)}, f32[64,1536]{1,0:T(8,128)}, u32[]{:S(2)}, u32[]{:S(2)}) collective-permute-start(f32[64,1536]{1,0:T(8,128)S(1)} %get-tuple-element.5.refs_1_), channel_id=1, source_target_pairs={{0,16},{8,24},{16,0},{24,8},{1,17},{9,25},{17,1},{25,9},{2,18},{10... | collective-permute-start | bytes 1179656 | tf_op jit(solution)/shard_map/ppermute | solution.py:184
  87.0 120.2 %copy-start = (bf16[1536,256]{1,0:T(8,128)(2,1)S(1)}, bf16[1536,256]{1,0:T(8,128)(2,1)}, u32[]{:S(2)}) copy-start(bf16[1536,256]{1,0:T(8,128)(2,1)} %constant.61.clone.refs_4_.refs_3_) | copy-start | bytes 2359300
  87.0 120.2 %copy-start.2 = (bf16[768,512]{1,0:T(8,128)(2,1)S(1)}, bf16[768,512]{1,0:T(8,128)(2,1)}, u32[]{:S(2)}) copy-start(bf16[768,512]{1,0:T(8,128)(2,1)} %constant.60.clone.refs_3_.refs_2_) | copy-start | bytes 2359300
  87.0 119.4 %collective-permute-start.3 = (f32[64,1536]{1,0:T(8,128)S(1)}, f32[64,1536]{1,0:T(8,128)S(1)}, u32[]{:S(2)}, u32[]{:S(2)}) collective-permute-start(f32[64,1536]{1,0:T(8,128)S(1)} %get-tuple-element.5.refs_1_), channel_id=1, source_target_pairs={{0,24},{8,0},{16,8},{24,16},{1,25},{9,1},{17,9},{25,17},{2,26},{10... | collective-permute-start | bytes 1179656 | tf_op jit(solution)/shard_map/ppermute | solution.py:184
  226.4 41.0 %all-to-all-start.2 = ((f32[4,256,768]{2,1,0:T(8,128)}), f32[4,256,768]{2,1,0:T(8,128)}, u32[]{:S(2)}, u32[]{:S(2)}) async-start(f32[4,256,768]{2,1,0:T(8,128)} %shard_map.86), calls=%async_computation.2 | async-start | bytes 6291456 | tf_op jit(solution)/shard_map/all_to_all | solution.py:194
  232.2 1.1 copy-start.1
  233.3 1.1 copy-start.3
